TPU v7x, 32 devices: a whole 2x2x4 slice. The times are simulated.
32 devices in a mesh: slab: 32 (over z, y, x, core).
Axes of the slice: x: 2, y: 2, z: 4, core: 2. Of those that a mesh axis runs over, the one named last changes fastest.
Arguments:
- series: float32 [80, 1048576], P(None, 'slab'), as said below
- noise_mask: int32 [1048576], P('slab'), may hold values 0 or 1
- probes: float32 [80, 5], replicated, may hold values from -6 to 6
- sample_weights: bfloat16 [1536, 256, 128], P('slab'), may hold values from -0.375 to 0.375
- block_ids: int32 [1536], P('slab'), may hold values from 0 to 127
- tile_ids: int32 [1536], P('slab'), may hold values from -1 to 127, as said below
- tile_owner: int32 [128], replicated, may hold values from 0 to 31, as said below
Outputs:
- vertex_series: float32 [128, 80, 128], P('slab')
Inputs may be any that keep to these rules, and one draw needn't show every extreme that they name: `tile_ids`: on each device the used entries come first and are at least half of its 48 entries; some device uses all. Used entry k of the device with index d names vertex tile (d * 4 + o_d + k) mod 128, with o_d in [0, 4) fixed per device; unused entries hold -1. tile_owner[j] = p[j mod the number of devices] for a permutation p of the devices, so every device owns 4 tiles. `series`: values of order one to some tens; each voxel carries its own baseline.
All inputs are finite; a program needn't handle non-finite values. No bound on the sum of `noise_mask` on one device may be relied on, other than what follows from the above.
Results may differ from a plain program's by a relative error of at most 0.005.
Values may be sent and summed in bfloat16 or wider, within the bound.
No kernel may reach another device: no remote copies, remote signals or barrier semaphores. Data moves between devices by JAX's collectives and lax.ppermute only.
A program may use at most 128 MiB of HBM per device.

v0:
```python
import jax
import jax.numpy as jnp
from jax import lax
from jax.sharding import PartitionSpec as P

HIGHEST = lax.Precision.HIGHEST


def make_projector(components):
    inner = jnp.dot(components.T, components, precision=HIGHEST)
    factor = jnp.linalg.cholesky(inner)
    solved = jax.scipy.linalg.cho_solve((factor, True), components.T)
    return jnp.dot(components, solved, precision=HIGHEST)


def body(series, noise_mask, probes, sample_weights, block_ids, tile_ids, tile_owner):
    frames, voxels = series.shape
    devices = lax.axis_size("slab")
    tile_width = sample_weights.shape[2]
    block_width = sample_weights.shape[1]
    owned = tile_owner.shape[0] // devices
    demeaned = series - jnp.mean(series, axis=0, keepdims=True)
    weighted = demeaned * noise_mask.astype(jnp.float32)[None, :]
    local_gram = lax.dot_general(weighted, demeaned, (((1,), (1,)), ((), ())), precision=HIGHEST)
    noise_gram = lax.psum(local_gram, "slab")
    components = jnp.dot(noise_gram, probes, precision=HIGHEST)
    projector = make_projector(components)
    cleaned = (demeaned - jnp.dot(projector, demeaned, precision=HIGHEST)).astype(jnp.bfloat16)
    blocks = cleaned.reshape(frames, voxels // block_width, block_width)
    picked = jnp.take(blocks, block_ids, axis=1)
    partial_value = jnp.einsum(
        "fkv,kvt->kft", picked, sample_weights, preferred_element_type=jnp.float32
    ).astype(jnp.bfloat16)
    used = tile_ids >= 0
    matches = tile_ids[:, None] == jnp.arange(tile_owner.shape[0], dtype=jnp.int32)[None, :]
    owners = jnp.sum(jnp.where(matches, tile_owner[None, :], 0), axis=1)
    local_slot = jnp.where(used, tile_ids // devices, -1)
    total_rows = owned * devices
    rows = jnp.where(used, owners * owned + local_slot, total_rows)
    widened = partial_value.astype(jnp.float32)
    inside = (rows >= 0) & (rows < owned * lax.axis_size("slab"))
    target = jnp.where(inside, rows, owned * lax.axis_size("slab"))
    empty = jnp.zeros((owned * lax.axis_size("slab"), frames, tile_width), jnp.float32)
    return lax.psum_scatter(
        empty.at[target].add(widened, mode="drop"), "slab", scatter_dimension=0, tiled=True
    )


def solution(mesh):
    return jax.shard_map(
        body,
        mesh=mesh,
        in_specs=(
            P(None, "slab"),
            P("slab"),
            P(),
            P("slab", None, None),
            P("slab"),
            P("slab"),
            P(),
        ),
        out_specs=P("slab", None, None),
        check_vma=False,
    )
```

profile of v0, /device:TPU:0, one launch (start us, length us, event | category | flops | bytes accessed | tf_op | source)
XLA Modules:
  0.0 259.4 jit_solution(14531749879565290467)
XLA Ops:
  6.5 0.0 copy-start
  6.5 0.0 reduce-scatter.2.cloned.1.call-start
  6.5 0.8 compare_and_fusion
  7.4 0.8 compare_select_fusion
  8.2 0.8 select_reduce_fusion
  9.0 0.7 compare_select_fusion.1
  9.7 0.9 convert_element_type.12
  10.6 4.7 %reduce_sum.19 = f32[32768]{0:T(1024)S(1)} reduce(f32[80,32768]{1,0:T(8,128)} %param.7, f32[]{:T(128)} %constant.78.clone.1), dimensions={0}, to_apply=%region_1.0 | reduce | flops 2588672 | bytes 10616836 | tf_op jit(solution)/shard_map/reduce_sum | solution.py:22
  15.3 0.0 copy-start.1
  15.3 13.9 %fusion.1 = f32[80,80]{1,0:T(8,128)S(1)} fusion(f32[80,32768]{1,0:T(8,128)} %param.7, f32[32768]{0:T(1024)S(1)} %convert_element_type.12, f32[32768]{0:T(1024)S(1)} %broadcast_multiply_fusion), kind=kOutput, calls=%fused_computation.4 | convolution fusion | flops 2524446720 | bytes 10773504 | tf_op jit(solution)/shard_map/dot_general | solution.py:24
  29.2 42.6 %psum.7 = f32[80,80]{1,0:T(8,128)S(1)} all-reduce(f32[80,80]{1,0:T(8,128)S(1)} %fusion.1), channel_id=1, replica_groups=mesh['slab'=32] {'slab'}, use_global_device_ids=true, to_apply=%region_2.3 | all-reduce | flops 6400 | bytes 51200 | tf_op jit(solution)/shard_map/psum | solution.py:25
  71.8 0.0 copy-done.1
  71.8 0.2 fusion.27
  71.9 0.2 fusion.28
  72.1 0.1 copy.13
  72.2 0.4 cholesky.16
  72.6 0.1 select_reduce_fusion.1
  72.7 0.6 compare_reduce_fusion
  73.3 0.6 fusion.19
  74.0 0.4 custom-call.10
  74.4 0.2 fusion.20
  74.6 0.1 fusion.22
  74.7 0.3 fusion.29
  75.0 12.9 %fusion = bf16[80,32768]{1,0:T(8,128)(2,1)S(1)} fusion(f32[80,80]{1,0:T(8,128)S(1)} %fusion.29, f32[80,32768]{1,0:T(8,128)} %param.7, f32[32768]{0:T(1024)S(1)} %broadcast_multiply_fusion), kind=kOutput, calls=%fused_computation.3 | convolution fusion | flops 2524446720 | bytes 15885312 | tf_op jit(solution)/shard_map/dot_general | solution.py:28
  87.9 2.8 %copy.18 = bf16[10,128,8,256]{3,2,0,1:T(8,128)(2,1)} copy(bf16[10,128,8,256]{3,2,1,0:T(8,128)(2,1)S(1)} %bitcast.34) | data formatting | bytes 10485760 | tf_op jit(solution)/shard_map/reshape | solution.py:29
  90.7 4.5 %gather_fusion = bf16[48,80,256]{2,1,0:T(8,128)(2,1)} fusion(bf16[80,128,256]{2,0,1:T(8,128)(2,1)} %bitcast.35, s32[1024]{0:T(1024)S(1)} %pad_clamp_fusion), kind=kCustom, calls=%fused_computation | custom fusion | bytes 3932352 | tf_op jit(solution)/shard_map/jit(_take)/gather | solution.py:30
  95.2 0.0 copy-done
  95.2 3.7 %fusion.15 = f32[48,80,128]{2,1,0:T(8,128)} fusion(bf16[48,256,128]{2,1,0:T(8,128)(2,1)S(1)} %copy-done, bf16[48,80,256]{2,1,0:T(8,128)(2,1)} %gather_fusion, pred[48]{0:T(512)(128)(4,1)S(1)} %compare_and_fusion), kind=kOutput, calls=%fused_computation.17 | convolution fusion | flops 253624320 | bytes 7077936 | tf_op jit(solution)/shard_map/fkv,kvt->kft/dot_general | solution.py:31
  98.9 2.7 %broadcast_in_dim.41 = f32[128,80,128]{2,1,0:T(8,128)} broadcast(f32[]{:T(128)} %constant.78.clone.1), dimensions={} | broadcast | bytes 5242884 | tf_op jit(solution)/shard_map/broadcast_in_dim | solution.py:43
  101.5 8.2 %scatter_fusion = f32[128,80,128]{2,1,0:T(8,128)} fusion(f32[128,80,128]{2,1,0:T(8,128)} %broadcast_in_dim.41, s32[48]{0:T(128)S(1)} %compare_select_fusion.1, f32[48,80,128]{2,1,0:T(8,128)} %fusion.15), kind=kCustom, calls=%fused_computation.1 | custom fusion | flops 491520 | bytes 5898432 | tf_op jit(solution)/shard_map/scatter-add | solution.py:45
  109.8 0.0 reduce-scatter.2.cloned.1.call-update
  109.8 142.7 %reduce-scatter.2.cloned.1.call-done = f32[4,80,128]{2,1,0:T(8,128)} async-done(((f32[128,80,128]{2,1,0:T(8,128)}), f32[4,80,128]{2,1,0:T(8,128)}) %reduce-scatter.2.cloned.1.call-update) | async-done | bytes 163856 | tf_op jit(solution)/shard_map/reduce_scatter | solution.py:44
  (3 shorter events, 0.0 us)
Async XLA Ops:
  6.5 88.7 %copy-start = (bf16[48,256,128]{2,1,0:T(8,128)(2,1)S(1)}, bf16[48,256,128]{2,1,0:T(8,128)(2,1)}, u32[]{:S(2)}) copy-start(bf16[48,256,128]{2,1,0:T(8,128)(2,1)} %param.10) | copy-start | bytes 9437188
  6.5 246.0 %reduce-scatter.2.cloned.1.call-start = ((), (), s32[]{:S(2)}) async-start(), calls=%async_computation.1 | async-start | bytes 5406720 | tf_op jit(solution)/shard_map/reduce_scatter | solution.py:44
  15.3 56.5 %copy-start.1 = (f32[80,5]{0,1:T(8,128)S(1)}, f32[80,5]{0,1:T(8,128)}, u32[]{:S(2)}) copy-start(f32[80,5]{0,1:T(8,128)} %param.9) | copy-start | bytes 4804
Sparse Core Ops, SparseCore 0:
  109.9 142.5 reduce-scatter.1
where the time goes:
time: 260 us; the launch traced here: 259 us
  waiting for transfers between devices  143 us (55%)
  blocking collectives  42.6 us (16%)
  matrix products  31.4 us (12%)
  other arithmetic  19.2 us (7%)
  between operations  13.5 us (5%)
  local copies, waits for them, and re-layouts  10 us (4%)
    reduce_scatter x1, waiting for transfers between devices, body(): lax.psum_scatter(empty.at[target].add(widened, mode='drop'), 'slab', scat...  143 us
    psum x1, blocking collectives, body(): noise_gram = lax.psum(local_gram, 'slab')  42.6 us
    dot_general x1, matrix products, body(): lax.dot_general(weighted, demeaned, (((1,), (1,)), ((), ())), precision=H...  13.9 us
    dot_general x1, matrix products, body(): jnp.dot(projector, demeaned, precision=HIGHEST)  12.9 us
    scatter-add x1, other arithmetic, body(): empty.at[target].add(widened, mode='drop')  8.25 us
  transfers between devices with their start and end apart: 1, of which 1 were waited for; matrix products, arithmetic and copies ran while one was open for 0% of the time, Pallas kernels for 0%

commit v1 on v0

--- a/solution.py
+++ b/solution.py
@@ -4,6 +4,14 @@
 from jax.sharding import PartitionSpec as P
 
 HIGHEST = lax.Precision.HIGHEST
+
+
+def add_in_pairs(x, mesh_axis):
+    size, total = (lax.axis_size(mesh_axis), x)
+    for hop in [1 << k for k in range(size.bit_length() - 1)]:
+        pairs = [(i, i ^ hop) for i in range(size)]
+        total = total + lax.ppermute(total, mesh_axis, pairs)
+    return total
 
 
 def make_projector(components):
@@ -22,7 +30,7 @@
     demeaned = series - jnp.mean(series, axis=0, keepdims=True)
     weighted = demeaned * noise_mask.astype(jnp.float32)[None, :]
     local_gram = lax.dot_general(weighted, demeaned, (((1,), (1,)), ((), ())), precision=HIGHEST)
-    noise_gram = lax.psum(local_gram, "slab")
+    noise_gram = add_in_pairs(local_gram, "slab")
     components = jnp.dot(noise_gram, probes, precision=HIGHEST)
     projector = make_projector(components)
     cleaned = (demeaned - jnp.dot(projector, demeaned, precision=HIGHEST)).astype(jnp.bfloat16)

time: 260 us -> 236 us (0.908)
  blocking collectives: 42.6 us -> 0 us
  waiting for transfers between devices: 143 us -> 154 us
  starting transfers between devices: 0.01 us -> 10.6 us
  other arithmetic: 19.2 us -> 16.4 us
    psum x1 -> x0, blocking collectives: 42.6 us -> none  [body(): noise_gram = lax.psum(local_gram, 'slab')]
    ppermute x0 -> x5, starting transfers between devices: none -> 10.6 us  [add_in_pairs(): total = total + lax.ppermute(total, mesh_axis, pairs)]
    ppermute x0 -> x5, waiting for transfers between devices: none -> 8.57 us  [add_in_pairs(): total = total + lax.ppermute(total, mesh_axis, pairs)]
  transfers between devices with their start and end apart: 1 -> 6, of which waited for: 1 -> 6; matrix products, arithmetic and copies ran while one was open for 0% -> 0% of each run, Pallas kernels for 0% -> 0%
where the time goes in v1:
time: 236 us
  waiting for transfers between devices  154 us (65%)
  matrix products  31.6 us (13%)
  other arithmetic  16.4 us (7%)
  between operations  13.5 us (6%)
  starting transfers between devices  10.6 us (4%)
  local copies, waits for them, and re-layouts  10.1 us (4%)
    reduce_scatter x1, waiting for transfers between devices, body(): lax.psum_scatter(empty.at[target].add(widened, mode='drop'), 'slab', scat...  145 us
    dot_general x1, matrix products, body(): lax.dot_general(weighted, demeaned, (((1,), (1,)), ((), ())), precision=H...  13.9 us
    dot_general x1, matrix products, body(): jnp.dot(projector, demeaned, precision=HIGHEST)  13.1 us
    ppermute x5, starting transfers between devices, add_in_pairs(): total = total + lax.ppermute(total, mesh_axis, pairs)  10.6 us
    ppermute x5, waiting for transfers between devices, add_in_pairs(): total = total + lax.ppermute(total, mesh_axis, pairs)  8.57 us
    scatter-add x1, other arithmetic, body(): empty.at[target].add(widened, mode='drop')  8.25 us
  transfers between devices with their start and end apart: 6, of which 6 were waited for; matrix products, arithmetic and copies ran while one was open for 0% of the time, Pallas kernels for 0%

profile of v1, /device:TPU:0, one launch (start us, length us, event | category | flops | bytes accessed | tf_op | source)
XLA Modules:
  0.0 236.0 jit_solution(5771365312990590895)
XLA Ops:
  6.5 0.0 copy-start
  6.5 0.0 reduce-scatter.2.cloned.1.call-start
  6.5 1.1 convert_element_type.12
  7.6 4.7 %reduce_sum.19 = f32[32768]{0:T(1024)S(1)} reduce(f32[80,32768]{1,0:T(8,128)} %param.7, f32[]{:T(128)} %constant.78.clone.1), dimensions={0}, to_apply=%region_1.2 | reduce | flops 2588672 | bytes 10616836 | tf_op jit(solution)/shard_map/reduce_sum | solution.py:30
  12.3 0.0 copy-start.2
  12.3 0.0 copy-start.3
  12.3 0.0 copy-start.4
  12.3 0.0 copy-start.1
  12.3 13.9 %fusion.1 = f32[80,80]{1,0:T(8,128)S(1)} fusion(f32[80,32768]{1,0:T(8,128)} %param.7, f32[32768]{0:T(1024)S(1)} %convert_element_type.12, f32[32768]{0:T(1024)S(1)} %broadcast_multiply_fusion), kind=kOutput, calls=%fused_computation.4 | convolution fusion | flops 2524446720 | bytes 10773504 | tf_op jit(solution)/shard_map/dot_general | solution.py:32
  26.2 0.5 collective-permute-start
  26.8 0.0 copy-done.2
  26.8 0.0 copy-done.3
  26.8 0.2 select_reduce_fusion
  26.9 0.7 collective-permute-done
  27.6 2.8 %collective-permute-start.1 = (f32[80,80]{1,0:T(8,128)S(1)}, f32[80,80]{1,0:T(8,128)S(1)}, u32[]{:S(2)}, u32[]{:S(2)}) collective-permute-start(f32[80,80]{1,0:T(8,128)S(1)} %add.50), channel_id=1, source_target_pairs={{0,2},{1,3},{2,0},{3,1},{4,6},{5,7},{6,4},{7,5},{8,10},{9,11},{10,... | collective-permute-start | bytes 76808 | tf_op jit(solution)/shard_map/ppermute | solution.py:13
  30.5 2.0 collective-permute-done.1
  32.5 2.1 collective-permute-start.2
  34.5 0.0 copy-done.4
  34.5 2.0 collective-permute-done.2
  36.5 2.1 collective-permute-start.3
  38.6 2.0 collective-permute-done.3
  40.6 3.1 %collective-permute-start.4 = (f32[80,80]{1,0:T(8,128)S(1)}, f32[80,80]{1,0:T(8,128)S(1)}, u32[]{:S(2)}, u32[]{:S(2)}) collective-permute-start(f32[80,80]{1,0:T(8,128)S(1)} %add.53), channel_id=1, source_target_pairs={{0,16},{1,17},{2,18},{3,19},{4,20},{5,21},{6,22},{7,23},{8,24},{9,... | collective-permute-start | bytes 76808 | tf_op jit(solution)/shard_map/ppermute | solution.py:13
  43.7 2.0 collective-permute-done.4
  45.6 0.0 copy-done.1
  45.7 0.2 fusion.19
  45.8 0.2 fusion.29
  46.0 0.1 copy.13
  46.1 0.4 cholesky.16
  46.5 0.1 select_reduce_fusion.1
  46.6 0.6 compare_reduce_fusion
  47.2 0.6 fusion.21
  47.9 0.4 custom-call.10
  48.3 0.2 fusion.22
  48.4 0.1 fusion.24
  48.6 0.3 fusion.30
  48.9 13.1 %fusion = bf16[80,32768]{1,0:T(8,128)(2,1)S(1)} fusion(f32[80,80]{1,0:T(8,128)S(1)} %fusion.30, f32[80,32768]{1,0:T(8,128)} %param.7, f32[32768]{0:T(1024)S(1)} %broadcast_multiply_fusion), kind=kOutput, calls=%fused_computation.3 | convolution fusion | flops 2524446720 | bytes 15885312 | tf_op jit(solution)/shard_map/dot_general | solution.py:36
  62.0 2.8 %copy.18 = bf16[10,128,8,256]{3,2,0,1:T(8,128)(2,1)} copy(bf16[10,128,8,256]{3,2,1,0:T(8,128)(2,1)S(1)} %bitcast.33) | data formatting | bytes 10485760 | tf_op jit(solution)/shard_map/reshape | solution.py:37
  64.7 4.5 %gather_fusion = bf16[48,80,256]{2,1,0:T(8,128)(2,1)} fusion(bf16[80,128,256]{2,0,1:T(8,128)(2,1)} %bitcast.34, s32[1024]{0:T(1024)S(1)} %pad_clamp_fusion), kind=kCustom, calls=%fused_computation | custom fusion | bytes 3932352 | tf_op jit(solution)/shard_map/jit(_take)/gather | solution.py:38
  69.3 0.0 copy-done
  69.3 3.7 %fusion.15 = f32[48,80,128]{2,1,0:T(8,128)} fusion(bf16[48,256,128]{2,1,0:T(8,128)(2,1)S(1)} %copy-done, bf16[48,80,256]{2,1,0:T(8,128)(2,1)} %gather_fusion, pred[48]{0:T(512)(128)(4,1)S(1)} %compare_and_fusion), kind=kOutput, calls=%fused_computation.17 | convolution fusion | flops 253624320 | bytes 7077936 | tf_op jit(solution)/shard_map/fkv,kvt->kft/dot_general | solution.py:39
  72.9 2.7 %broadcast_in_dim.41 = f32[128,80,128]{2,1,0:T(8,128)} broadcast(f32[]{:T(128)} %constant.78.clone.1), dimensions={} | broadcast | bytes 5242884 | tf_op jit(solution)/shard_map/broadcast_in_dim | solution.py:51
  75.6 8.2 %scatter_fusion = f32[128,80,128]{2,1,0:T(8,128)} fusion(f32[128,80,128]{2,1,0:T(8,128)} %broadcast_in_dim.41, s32[48]{0:T(128)S(1)} %compare_select_fusion.1, f32[48,80,128]{2,1,0:T(8,128)} %fusion.15), kind=kCustom, calls=%fused_computation.1 | custom fusion | flops 491520 | bytes 5898432 | tf_op jit(solution)/shard_map/scatter-add | solution.py:53
  83.9 0.0 reduce-scatter.2.cloned.1.call-update
  83.9 145.3 %reduce-scatter.2.cloned.1.call-done = f32[4,80,128]{2,1,0:T(8,128)} async-done(((f32[128,80,128]{2,1,0:T(8,128)}), f32[4,80,128]{2,1,0:T(8,128)}) %reduce-scatter.2.cloned.1.call-update) | async-done | bytes 163856 | tf_op jit(solution)/shard_map/reduce_scatter | solution.py:52
  (10 shorter events, 0.1 us)
Async XLA Ops:
  6.5 62.7 %copy-start = (bf16[48,256,128]{2,1,0:T(8,128)(2,1)S(1)}, bf16[48,256,128]{2,1,0:T(8,128)(2,1)}, u32[]{:S(2)}) copy-start(bf16[48,256,128]{2,1,0:T(8,128)(2,1)} %param.10) | copy-start | bytes 9437188
  6.5 222.6 %reduce-scatter.2.cloned.1.call-start = ((), (), s32[]{:S(2)}) async-start(), calls=%async_computation.1 | async-start | bytes 5406720 | tf_op jit(solution)/shard_map/reduce_scatter | solution.py:52
  12.3 14.5 %copy-start.2 = (s32[128]{0:T(128)S(1)}, s32[128]{0:T(128)}, u32[]{:S(2)}) copy-start(s32[128]{0:T(128)} %param.13) | copy-start | bytes 1540
  12.3 14.4 %copy-start.3 = (s32[48]{0:T(128)S(1)}, s32[48]{0:T(128)}, u32[]{:S(2)}) copy-start(s32[48]{0:T(128)} %param.12) | copy-start | bytes 580
  12.3 22.2 %copy-start.4 = (s32[48]{0:T(128)S(1)}, s32[48]{0:T(128)}, u32[]{:S(2)}) copy-start(s32[48]{0:T(128)} %param.11) | copy-start | bytes 580
  12.3 33.3 %copy-start.1 = (f32[80,5]{0,1:T(8,128)S(1)}, f32[80,5]{0,1:T(8,128)}, u32[]{:S(2)}) copy-start(f32[80,5]{0,1:T(8,128)} %param.9) | copy-start | bytes 4804
  26.2 1.4 collective-permute-start
  27.6 4.8 %collective-permute-start.1 = (f32[80,80]{1,0:T(8,128)S(1)}, f32[80,80]{1,0:T(8,128)S(1)}, u32[]{:S(2)}, u32[]{:S(2)}) collective-permute-start(f32[80,80]{1,0:T(8,128)S(1)} %add.50), channel_id=1, source_target_pairs={{0,2},{1,3},{2,0},{3,1},{4,6},{5,7},{6,4},{7,5},{8,10},{9,11},{10,... | collective-permute-start | bytes 76808 | tf_op jit(solution)/shard_map/ppermute | solution.py:13
  32.5 4.0 %collective-permute-start.2 = (f32[80,80]{1,0:T(8,128)S(1)}, f32[80,80]{1,0:T(8,128)S(1)}, u32[]{:S(2)}, u32[]{:S(2)}) collective-permute-start(f32[80,80]{1,0:T(8,128)S(1)} %add.51), channel_id=1, source_target_pairs={{0,4},{1,5},{2,6},{3,7},{4,0},{5,1},{6,2},{7,3},{8,12},{9,13},{10,... | collective-permute-start | bytes 76808 | tf_op jit(solution)/shard_map/ppermute | solution.py:13
  36.5 4.1 %collective-permute-start.3 = (f32[80,80]{1,0:T(8,128)S(1)}, f32[80,80]{1,0:T(8,128)S(1)}, u32[]{:S(2)}, u32[]{:S(2)}) collective-permute-start(f32[80,80]{1,0:T(8,128)S(1)} %add.52), channel_id=1, source_target_pairs={{0,8},{1,9},{2,10},{3,11},{4,12},{5,13},{6,14},{7,15},{8,0},{9,1},... | collective-permute-start | bytes 76808 | tf_op jit(solution)/shard_map/ppermute | solution.py:13
  40.6 5.1 %collective-permute-start.4 = (f32[80,80]{1,0:T(8,128)S(1)}, f32[80,80]{1,0:T(8,128)S(1)}, u32[]{:S(2)}, u32[]{:S(2)}) collective-permute-start(f32[80,80]{1,0:T(8,128)S(1)} %add.53), channel_id=1, source_target_pairs={{0,16},{1,17},{2,18},{3,19},{4,20},{5,21},{6,22},{7,23},{8,24},{9,... | collective-permute-start | bytes 76808 | tf_op jit(solution)/shard_map/ppermute | solution.py:13
Sparse Core Ops, SparseCore 0:
  84.0 145.1 reduce-scatter.1
